TPU v7x, 32 devices: a whole 2x2x4 slice. The times are simulated.
32 devices in a mesh: beam: 2 (over x), rng: 16 (over z, y, core).
Axes of the slice: x: 2, y: 2, z: 4, core: 2. Of those that a mesh axis runs over, the one named last changes fastest.
Arguments:
- echoes: bfloat16 [4, 1024, 8192], P('beam', 'rng'), parts along dimension 0, may hold values from -6 to 6
- phase_code: int32 [256], replicated, may hold values from -1 to 1, as said below
Outputs:
- test_ratio: float32 [2048, 8192], P('beam', 'rng'), parts along dimension 0
There are 2 independent parts, one for each index of `beam`. A program takes and returns all parts, laid end to end along the dimension named above; an argument that names none is the same for every part. Nothing has to cross between parts.
Inputs may be any that keep to these rules, and one draw needn't show every extreme that they name: `phase_code`: each entry is -1 or +1.
All inputs are finite; a program needn't handle non-finite values.
Results may differ from a plain program's by a relative error of at most 0.0039.
Values may be sent and summed in bfloat16 or wider, within the bound.
A program may use at most 128 MiB of HBM per device.

v0:
```python
import math
import jax
import jax.numpy as jnp
from jax import lax
from jax.sharding import PartitionSpec as P

WIN_R = 33
WIN_D = 9
GUARD_R = 5
GUARD_D = 3


def extended(cells, sides, width):
    for axis, dim in sides:
        count = lax.axis_size(axis)
        ends = count - 1
        head = lax.slice_in_dim(cells, 0, width, axis=dim)
        tail = lax.slice_in_dim(cells, cells.shape[dim] - width, cells.shape[dim], axis=dim)
        cells = jnp.concatenate(
            [
                lax.ppermute(tail, axis, [(i, (i + 1) % count) for i in range(ends)]),
                cells,
                lax.ppermute(head, axis, [((i + 1) % count, i) for i in range(ends)]),
            ],
            axis=dim,
        )
    return cells


def toeplitz_pair(phase_code):
    length = phase_code.shape[0]
    values = phase_code.astype(jnp.float32)
    padded_code = jnp.concatenate([values, jnp.zeros((length,), jnp.float32)])
    rotated = jnp.roll(padded_code, length - 1)
    repeated = jnp.tile(rotated, length + 1)[: length * (2 * length + 1)]
    rows_made = repeated.reshape(length, 2 * length + 1)[:, : 2 * length]
    return rows_made[::-1].T.astype(jnp.bfloat16)


def compress_rows(echo_rows, next_tail, filter_pair):
    length = filter_pair.shape[1]
    row_count = echo_rows.shape[0]
    cell_count = echo_rows.shape[1]
    blocks = cell_count // length
    upper_half = filter_pair[:length]
    lower_half = filter_pair[length:]
    block_rows = echo_rows.reshape(row_count * blocks, length)
    own_terms = jnp.dot(block_rows, upper_half, preferred_element_type=jnp.float32).reshape(
        row_count, blocks, length
    )
    next_terms = jnp.dot(block_rows, lower_half, preferred_element_type=jnp.float32).reshape(
        row_count, blocks, length
    )
    tail_terms = jnp.dot(next_tail, lower_half, preferred_element_type=jnp.float32).reshape(
        row_count, 1, length
    )
    result = own_terms + jnp.concatenate([next_terms[:, 1:], tail_terms], axis=1)
    return result.reshape(row_count, cell_count).astype(jnp.bfloat16)


def doppler_table(pulses):
    index_all = jnp.arange(pulses, dtype=jnp.int32)
    phase_angle = (index_all[:, None] * index_all[None, :] % pulses).astype(jnp.float32) * (
        2.0 * math.pi / pulses
    )
    window_taper = 0.5 - 0.5 * jnp.cos(
        (index_all.astype(jnp.float32) + 0.5) * (2.0 * math.pi / pulses)
    )
    cosine = window_taper[None, :] * jnp.cos(phase_angle)
    sine_part = window_taper[None, :] * jnp.sin(phase_angle)
    top_rows = jnp.concatenate([cosine, sine_part], axis=1)
    bottom_rows = jnp.concatenate([-sine_part, cosine], axis=1)
    return jnp.concatenate([top_rows, bottom_rows], axis=0).astype(jnp.bfloat16)


def power_of(table, compressed):
    pulses = compressed.shape[1]
    stacked = compressed.reshape(2 * pulses, compressed.shape[2])
    spectrum = jnp.dot(table, stacked, preferred_element_type=jnp.float32)
    return spectrum[:pulses] * spectrum[:pulses] + spectrum[pulses:] * spectrum[pulses:]


def range_sums(padded, half_width, margin):
    cell_count = padded.shape[-1] - 2 * margin
    running = padded[..., margin - half_width : margin - half_width + cell_count]
    for offset in range(margin - half_width + 1, margin + half_width + 1):
        running = running + padded[..., offset : offset + cell_count]
    return running


def slice_sums(wrapped, half_width, reach, pulses):
    running = wrapped[reach - half_width : reach - half_width + pulses]
    for offset in range(reach - half_width + 1, reach + half_width + 1):
        running = running + wrapped[offset : offset + pulses]
    return running


def cfar_ratio(padded, valid_mask):
    margin = WIN_R // 2
    reach = WIN_D // 2
    pulses = padded.shape[0]
    wrapped = jnp.concatenate([padded[pulses - reach :], padded, padded[:reach]], axis=0)
    wide_sums = range_sums(wrapped, WIN_R // 2, margin)
    guard_sums = range_sums(wrapped, GUARD_R // 2, margin)
    train_sums = slice_sums(wide_sums, WIN_D // 2, reach, pulses) - slice_sums(
        guard_sums, GUARD_D // 2, reach, pulses
    )
    train_count = (
        range_sums(valid_mask, WIN_R // 2, margin) * WIN_D
        - range_sums(valid_mask, GUARD_R // 2, margin) * GUARD_D
    )
    noise_level = train_sums / train_count[None, :]
    center_power = padded[:, margin : padded.shape[1] - margin]
    return center_power / noise_level


def corner_turn(signal):
    return lax.all_to_all(signal, "rng", split_axis=2, concat_axis=1, tiled=True)


def local(echoes, phase_code):
    filter_pair = toeplitz_pair(phase_code)
    length = phase_code.shape[0]
    local_pulses = echoes.shape[1]
    all_cells = echoes.shape[2]
    local_rows = echoes.reshape(2 * local_pulses, all_cells)
    zero_tail = jnp.zeros((2 * local_pulses, length), jnp.bfloat16)
    local_compressed = compress_rows(local_rows, zero_tail, filter_pair).reshape(
        2, local_pulses, all_cells
    )
    compressed = corner_turn(local_compressed)
    pulses = compressed.shape[1]
    cell_count = compressed.shape[2]
    table = doppler_table(pulses)
    margin = WIN_R // 2
    power_map = power_of(table, compressed)
    padded = extended(power_map, (("rng", 1),), margin)
    position = (
        lax.axis_index("rng") * cell_count
        + jnp.arange(cell_count + 2 * margin, dtype=jnp.int32)
        - margin
    )
    total_cells = cell_count * lax.axis_size("rng")
    valid_mask = ((position >= 0) & (position < total_cells)).astype(jnp.float32)
    return cfar_ratio(padded, valid_mask)


def solution(mesh):
    placed = (P("beam", "rng", None), P())
    return jax.shard_map(
        local, mesh=mesh, in_specs=placed, out_specs=P("beam", "rng"), check_vma=False
    )
```

profile of v0, /device:TPU:13, one launch (start us, length us, event | category | flops | bytes accessed | tf_op | source)
XLA Modules:
  0.0 180.7 jit_solution(8680494630458086528)
XLA Ops:
  0.0 0.7 convert_element_type.41
  1.0 0.6 reshape.33
  1.6 0.3 rev.3
  1.9 2.9 %reshape_reshape.3 = bf16[4096,256]{1,0:T(8,128)(2,1)S(1)} reshape(bf16[2,64,8192]{2,1,0:T(8,128)(2,1)} %param.2) | data formatting | bytes 4194304 | tf_op jit(solution)/shard_map/reshape;reshape | solution.py:47
  5.0 2.7 %convolution_bitcast_fusion = f32[4096,256]{0,1:T(8,128)} fusion(bf16[4096,256]{1,0:T(8,128)(2,1)S(1)} %reshape_reshape.3, bf16[512,256]{0,1:T(8,128)(2,1)S(1)} %bitcast.26), kind=kOutput, calls=%fused_computation.11 | convolution fusion | flops 536870912 | bytes 6422528 | tf_op jit(solution)/shard_map/dot_general | solution.py:51
  7.7 2.7 %convolution_bitcast_fusion.1 = f32[4096,256]{0,1:T(8,128)} fusion(bf16[4096,256]{1,0:T(8,128)(2,1)S(1)} %reshape_reshape.3, bf16[512,256]{0,1:T(8,128)(2,1)S(1)} %bitcast.27), kind=kOutput, calls=%fused_computation.12 | convolution fusion | flops 536870912 | bytes 6422528 | tf_op jit(solution)/shard_map/dot_general | solution.py:48
  10.4 5.6 %copy.16 = f32[4096,256]{1,0:T(8,128)} copy(f32[4096,256]{0,1:T(8,128)} %convolution_bitcast_fusion) | data formatting | bytes 8388608 | tf_op jit(solution)/shard_map/dot_general | solution.py:51
  16.0 2.8 %slice.379 = f32[128,31,256]{2,1,0:T(8,128)S(1)} slice(f32[128,32,256]{2,1,0:T(8,128)} %bitcast.23), slice={[0:128], [1:32], [0:256]} | slice | bytes 8126464 | tf_op jit(solution)/shard_map/slice | solution.py:57
  18.9 2.5 %pad_maximum_fusion = f32[128,32,256]{2,1,0:T(8,128)} fusion(f32[128,1,256]{2,1,0:T(1,128)S(1)} %copy.17, f32[128,31,256]{2,1,0:T(8,128)S(1)} %slice.379), kind=kLoop, calls=%fused_computation.16 | loop fusion | flops 1048576 | bytes 8388608 | tf_op jit(solution)/shard_map/concatenate | solution.py:57
  21.5 5.0 %concatenate.36 = f32[2,64,8192]{2,1,0:T(8,128)} reshape(f32[128,32,256]{2,1,0:T(8,128)} %pad_maximum_fusion) | data formatting | bytes 8388608 | tf_op jit(solution)/shard_map/concatenate | solution.py:57
  26.4 5.6 %copy.15 = f32[4096,256]{1,0:T(8,128)} copy(f32[4096,256]{0,1:T(8,128)} %convolution_bitcast_fusion.1) | data formatting | bytes 8388608 | tf_op jit(solution)/shard_map/dot_general | solution.py:48
  32.1 4.9 %reshape.34 = f32[2,64,8192]{2,1,0:T(8,128)} reshape(f32[4096,256]{1,0:T(8,128)} %copy.15) | data formatting | bytes 8388608 | tf_op jit(solution)/shard_map/reshape | solution.py:48
  37.0 3.9 %add_convert_fusion = bf16[2,64,8192]{2,1,0:T(8,128)(2,1)S(1)} fusion(f32[2,64,8192]{2,1,0:T(8,128)} %reshape.34, f32[2,64,8192]{2,1,0:T(8,128)} %concatenate.36), kind=kLoop, calls=%fused_computation.17 | loop fusion | flops 2097152 | bytes 10485760 | tf_op jit(solution)/shard_map/convert_element_type | solution.py:58
  40.9 6.9 %copy.18 = bf16[2,64,8192]{1,0,2:T(2,128)(2,1)} copy(bf16[2,64,8192]{2,1,0:T(8,128)(2,1)S(1)} %add_convert_fusion) | data formatting | bytes 4194304 | tf_op jit(solution)/shard_map/convert_element_type | solution.py:58
  47.8 7.5 %reshape.38 = bf16[16,2,32768]{2,1,0:T(2,128)(2,1)} reshape(bf16[8192,2,64]{2,1,0:T(2,128)(2,1)} %bitcast.21) | data formatting | bytes 4194304
  55.3 6.6 %all-to-all-start = ((bf16[16,2,32768]{2,1,0:T(2,128)(2,1)}), bf16[16,2,32768]{2,1,0:T(2,128)(2,1)S(1)}, u32[]{:S(2)}, u32[]{:S(2)}) async-start(bf16[16,2,32768]{2,1,0:T(2,128)(2,1)} %reshape.38), calls=%async_computation | async-start | bytes 4194304 | tf_op jit(solution)/shard_map/all_to_all | solution.py:118
  61.9 19.0 %fusion.14 = (bf16[1024,1024]{1,0:T(8,128)(2,1)}, bf16[1024,1024]{1,0:T(8,128)(2,1)}, bf16[1024,1024]{1,0:T(8,128)(2,1)}) fusion(f32[1024]{0:T(1024)S(1)} %multiply_subtract_fusion), kind=kLoop, calls=%fused_computation.24 | loop fusion | flops 20971520 | bytes 6295552 | tf_op jit(solution)/shard_map/convert.5
  80.9 28.3 %all-to-all-done = bf16[16,2,32768]{2,1,0:T(2,128)(2,1)S(1)} async-done(((bf16[16,2,32768]{2,1,0:T(2,128)(2,1)}), bf16[16,2,32768]{2,1,0:T(2,128)(2,1)S(1)}, u32[]{:S(2)}, u32[]{:S(2)}) %all-to-all-start) | async-done | bytes 2097184 | tf_op jit(solution)/shard_map/all_to_all | solution.py:118
  109.3 5.0 %reshape.39 = bf16[8192,2,64]{2,1,0:T(2,128)(2,1)} reshape(bf16[16,2,32768]{2,1,0:T(2,128)(2,1)S(1)} %all-to-all-done) | data formatting | bytes 4194304
  114.2 9.1 %copy.23 = bf16[2,64,16,512]{3,1,2,0:T(8,128)(2,1)S(1)} copy(bf16[2,64,16,512]{1,0,3,2:T(2,128)(2,1)} %bitcast.22) | data formatting | bytes 4194304 | tf_op jit(solution)/shard_map/all_to_all | solution.py:118
  123.3 10.6 %fusion = f32[2048,512]{0,1:T(8,128)S(1)} fusion(bf16[2048,512]{1,0:T(8,128)(2,1)S(1)} %bitcast.24, bf16[1024,1024]{1,0:T(8,128)(2,1)} %get-tuple-element.11, bf16[1024,1024]{1,0:T(8,128)(2,1)} %get-tuple-element.10, bf16[1024,1024]{1,0:T(8,128)(2,1)} %get-tuple-element.9), kind=kOutput, calls=%fused_computation | convolution fusion | flops 4328521728 | bytes 12582912 | tf_op jit(solution)/shard_map/dot_general | solution.py:79
  133.9 0.4 fusion.22
  134.4 1.5 copy-done
  135.8 3.6 %collective-permute-start = (f32[1024,16]{0,1:T(8,128)S(1)}, f32[1024,16]{0,1:T(8,128)S(1)}, u32[]{:S(2)}, u32[]{:S(2)}) collective-permute-start(f32[1024,16]{0,1:T(8,128)S(1)} %get-tuple-element.7), channel_id=1, source_target_pairs={{0,1},{1,2},{2,3},{3,4},{4,5},{5,6},{6,7},{7,8},{8,9},{9,10},{10,1... | collective-permute-start | bytes 196616 | tf_op jit(solution)/shard_map/ppermute | solution.py:21
  139.4 2.1 %collective-permute-start.1 = (f32[1024,16]{0,1:T(8,128)S(1)}, f32[1024,16]{0,1:T(8,128)S(1)}, u32[]{:S(2)}, u32[]{:S(2)}) collective-permute-start(f32[1024,16]{0,1:T(8,128)S(1)} %get-tuple-element.8), channel_id=1, source_target_pairs={{1,0},{2,1},{3,2},{4,3},{5,4},{6,5},{7,6},{8,7},{9,8},{10,9},{11,1... | collective-permute-start | bytes 196616 | tf_op jit(solution)/shard_map/ppermute | solution.py:23
  141.7 4.2 %collective-permute-done.1 = f32[1024,16]{0,1:T(8,128)S(1)} collective-permute-done((f32[1024,16]{0,1:T(8,128)S(1)}, f32[1024,16]{0,1:T(8,128)S(1)}, u32[]{:S(2)}, u32[]{:S(2)}) %collective-permute-start.1) | collective-permute-done | bytes 65568 | tf_op jit(solution)/shard_map/ppermute | solution.py:23
  146.3 1.2 copy-done.1
  147.6 3.2 %concatenate.38 = f32[1032,544]{0,1:T(8,128)S(1)} concatenate(f32[4,544]{0,1:T(8,128)S(1)} %get-tuple-element.6, f32[1024,544]{0,1:T(8,128)} %copy-done.1, f32[4,544]{0,1:T(8,128)S(1)} %get-tuple-element.5), dimensions={0} | concatenate | bytes 4491264 | tf_op jit(solution)/shard_map/concatenate | solution.py:102
  150.7 2.3 %add_add_fusion = f32[1032,512]{0,1:T(8,128)} fusion(f32[1032,544]{0,1:T(8,128)S(1)} %concatenate.38), kind=kLoop, calls=%fused_computation.57 | loop fusion | flops 2113536 | bytes 12681216 | tf_op jit(solution)/shard_map/add | solution.py:87
  153.1 7.7 %slice_add_fusion = f32[1032,512]{0,1:T(8,128)} fusion(f32[1032,544]{0,1:T(8,128)S(1)} %concatenate.38), kind=kLoop, calls=%fused_computation.25 | loop fusion | flops 16908288 | bytes 71860224 | tf_op jit(solution)/shard_map/add | solution.py:87
  160.8 18.1 %fusion.21 = f32[1024,512]{0,1:T(8,128)S(1)} fusion(f32[1032,512]{0,1:T(8,128)} %add_add_fusion, f32[1032,512]{0,1:T(8,128)} %slice_add_fusion, f32[512]{0:T(512)S(1)} %multiply_subtract_fusion.1, f32[2048,512]{0,1:T(8,128)} %copy-done), kind=kLoop, calls=%fused_computation.61 | loop fusion | flops 8388608 | bytes 31459328 | tf_op jit(solution)/shard_map/div | solution.py:114
  178.8 1.8 %copy.21 = f32[1024,512]{1,0:T(8,128)} copy(f32[1024,512]{0,1:T(8,128)S(1)} %fusion.21) | data formatting | bytes 4194304 | tf_op jit(solution)/shard_map/div | solution.py:114
  (16 shorter events, 1.2 us)
Async XLA Ops:
  55.3 54.0 %all-to-all-start = ((bf16[16,2,32768]{2,1,0:T(2,128)(2,1)}), bf16[16,2,32768]{2,1,0:T(2,128)(2,1)S(1)}, u32[]{:S(2)}, u32[]{:S(2)}) async-start(bf16[16,2,32768]{2,1,0:T(2,128)(2,1)} %reshape.38), calls=%async_computation | async-start | bytes 4194304 | tf_op jit(solution)/shard_map/all_to_all | solution.py:118
  133.9 1.9 %copy-start = (f32[2048,512]{0,1:T(8,128)}, f32[2048,512]{0,1:T(8,128)S(1)}, u32[]{:S(2)}) copy-start(f32[2048,512]{0,1:T(8,128)S(1)} %fusion) | copy-start | bytes 12582916
  135.8 5.8 %collective-permute-start = (f32[1024,16]{0,1:T(8,128)S(1)}, f32[1024,16]{0,1:T(8,128)S(1)}, u32[]{:S(2)}, u32[]{:S(2)}) collective-permute-start(f32[1024,16]{0,1:T(8,128)S(1)} %get-tuple-element.7), channel_id=1, source_target_pairs={{0,1},{1,2},{2,3},{3,4},{4,5},{5,6},{6,7},{7,8},{8,9},{9,10},{10,1... | collective-permute-start | bytes 196616 | tf_op jit(solution)/shard_map/ppermute | solution.py:21
  139.4 6.5 %collective-permute-start.1 = (f32[1024,16]{0,1:T(8,128)S(1)}, f32[1024,16]{0,1:T(8,128)S(1)}, u32[]{:S(2)}, u32[]{:S(2)}) collective-permute-start(f32[1024,16]{0,1:T(8,128)S(1)} %get-tuple-element.8), channel_id=1, source_target_pairs={{1,0},{2,1},{3,2},{4,3},{5,4},{6,5},{7,6},{8,7},{9,8},{10,9},{11,1... | collective-permute-start | bytes 196616 | tf_op jit(solution)/shard_map/ppermute | solution.py:23
  146.2 1.4 copy-start.1
where the time goes:
time: 182 us; the launch traced here: 181 us
  local copies, waits for them, and re-layouts  64.4 us (35%)
  other arithmetic  55.1 us (30%)
  waiting for transfers between devices  32.5 us (18%)
  matrix products  16.1 us (9%)
  starting transfers between devices  12.3 us (7%)
    all_to_all x1, waiting for transfers between devices, corner_turn(): lax.all_to_all(signal, 'rng', split_axis=2, concat_axis=1, tiled=True)  28.3 us
    another operation x1, other arithmetic  19 us
    div x1, other arithmetic, cfar_ratio(): return center_power / noise_level  18.1 us
    unnamed x6, local copies, waits for them, and re-layouts  15.2 us
    dot_general x1, matrix products, power_of(): spectrum = jnp.dot(table, stacked, preferred_element_type=jnp.float32)  10.6 us
    add x2, other arithmetic, range_sums(): running = running + padded[..., offset:offset + cell_count]  10 us
    all_to_all x1, local copies, waits for them, and re-layouts, corner_turn(): lax.all_to_all(signal, 'rng', split_axis=2, concat_axis=1, tiled=True)  9.07 us
    convert_element_type x1, local copies, waits for them, and re-layouts, compress_rows(): return result.reshape(row_count, cell_count).astype(jnp.bfloat16)  6.89 us
  transfers between devices with their start and end apart: 3, of which 2 were waited for; matrix products, arithmetic and copies ran while one was open for 11% of the time, Pallas kernels for 0%

commit v1 on v0

--- a/solution.py
+++ b/solution.py
@@ -115,7 +115,15 @@
 
 
 def corner_turn(signal):
-    return lax.all_to_all(signal, "rng", split_axis=2, concat_axis=1, tiled=True)
+    return jnp.concatenate(
+        lax.all_to_all(
+            jnp.stack(jnp.split(signal, lax.axis_size("rng"), axis=2)),
+            axis_name="rng",
+            concat_axis=0,
+            split_axis=0,
+        ),
+        1,
+    )
 
 
 def local(echoes, phase_code):

time: 182 us -> 164 us (0.901)
  local copies, waits for them, and re-layouts: 64.4 us -> 46.7 us
    all_to_all x1 -> x0, local copies, waits for them, and re-layouts: 9.07 us -> none  [corner_turn(): lax.all_to_all(signal, 'rng', split_axis=2, concat_axis=1, tiled=True)]
    convert_element_type x1 -> x0, local copies, waits for them, and re-layouts: 6.89 us -> none  [compress_rows(): return result.reshape(row_count, cell_count).astype(jnp.bfloat16)]
    unnamed x6 -> x19, local copies, waits for them, and re-layouts: 15.2 us -> 12.7 us
  transfers between devices with their start and end apart: 3 -> 3, of which waited for: 2 -> 2; matrix products, arithmetic and copies ran while one was open for 11% -> 12% of each run, Pallas kernels for 0% -> 0%
where the time goes in v1:
time: 164 us; the launch traced here: 163 us
  other arithmetic  55.1 us (34%)
  local copies, waits for them, and re-layouts  46.7 us (28%)
  waiting for transfers between devices  32.5 us (20%)
  matrix products  16.3 us (10%)
  starting transfers between devices  12.3 us (8%)
    all_to_all x1, waiting for transfers between devices, corner_turn(): lax.all_to_all(jnp.stack(jnp.split(signal, lax.axis_size('rng'), axis=2))...  28.3 us
    another operation x1, other arithmetic  19 us
    div x1, other arithmetic, cfar_ratio(): return center_power / noise_level  18.1 us
    unnamed x19, local copies, waits for them, and re-layouts  12.7 us
    dot_general x1, matrix products, power_of(): spectrum = jnp.dot(table, stacked, preferred_element_type=jnp.float32)  10.7 us
    add x2, other arithmetic, range_sums(): running = running + padded[..., offset:offset + cell_count]  10 us
    all_to_all x1, starting transfers between devices, corner_turn(): lax.all_to_all(jnp.stack(jnp.split(signal, lax.axis_size('rng'), axis=2))...  6.56 us
    dot_general x1, local copies, waits for them, and re-layouts, compress_rows(): jnp.dot(block_rows, lower_half, preferred_element_type=jnp.float32)  5.61 us
  transfers between devices with their start and end apart: 3, of which 2 were waited for; matrix products, arithmetic and copies ran while one was open for 12% of the time, Pallas kernels for 0%

profile of v1, /device:TPU:13, one launch (start us, length us, event | category | flops | bytes accessed | tf_op | source)
XLA Modules:
  0.0 163.1 jit_solution(352833490076749083)
XLA Ops:
  0.0 0.7 convert_element_type.41
  1.9 2.9 %reshape_reshape.6 = bf16[4096,256]{1,0:T(8,128)(2,1)S(1)} reshape(bf16[2,64,8192]{2,1,0:T(8,128)(2,1)} %param.2) | data formatting | bytes 4194304 | tf_op jit(solution)/shard_map/reshape;reshape | solution.py:47
  5.0 2.7 %convolution_bitcast_fusion = f32[4096,256]{0,1:T(8,128)} fusion(bf16[4096,256]{1,0:T(8,128)(2,1)S(1)} %reshape_reshape.6, bf16[512,256]{0,1:T(8,128)(2,1)S(1)} %bitcast.84), kind=kOutput, calls=%fused_computation.11 | convolution fusion | flops 536870912 | bytes 6422528 | tf_op jit(solution)/shard_map/dot_general | solution.py:51
  7.7 2.7 %convolution_bitcast_fusion.1 = f32[4096,256]{0,1:T(8,128)} fusion(bf16[4096,256]{1,0:T(8,128)(2,1)S(1)} %reshape_reshape.6, bf16[512,256]{0,1:T(8,128)(2,1)S(1)} %bitcast.85), kind=kOutput, calls=%fused_computation.12 | convolution fusion | flops 536870912 | bytes 6422528 | tf_op jit(solution)/shard_map/dot_general | solution.py:48
  10.4 5.6 %copy.6 = f32[4096,256]{1,0:T(8,128)} copy(f32[4096,256]{0,1:T(8,128)} %convolution_bitcast_fusion) | data formatting | bytes 8388608 | tf_op jit(solution)/shard_map/dot_general | solution.py:51
  16.0 2.8 %slice.379 = f32[128,31,256]{2,1,0:T(8,128)S(1)} slice(f32[128,32,256]{2,1,0:T(8,128)} %bitcast.80), slice={[0:128], [1:32], [0:256]} | slice | bytes 8126464 | tf_op jit(solution)/shard_map/slice | solution.py:57
  18.9 2.5 %pad_maximum_fusion = f32[128,32,256]{2,1,0:T(8,128)} fusion(f32[128,1,256]{2,1,0:T(1,128)S(1)} %copy.7, f32[128,31,256]{2,1,0:T(8,128)S(1)} %slice.379), kind=kLoop, calls=%fused_computation.16 | loop fusion | flops 1048576 | bytes 8388608 | tf_op jit(solution)/shard_map/concatenate | solution.py:57
  21.5 5.0 %concatenate.36 = f32[2,64,8192]{2,1,0:T(8,128)} reshape(f32[128,32,256]{2,1,0:T(8,128)} %pad_maximum_fusion) | data formatting | bytes 8388608 | tf_op jit(solution)/shard_map/concatenate | solution.py:57
  26.4 5.6 %copy.5 = f32[4096,256]{1,0:T(8,128)} copy(f32[4096,256]{0,1:T(8,128)} %convolution_bitcast_fusion.1) | data formatting | bytes 8388608 | tf_op jit(solution)/shard_map/dot_general | solution.py:48
  32.1 4.9 %reshape.33 = f32[2,64,8192]{2,1,0:T(8,128)} reshape(f32[4096,256]{1,0:T(8,128)} %copy.5) | data formatting | bytes 8388608 | tf_op jit(solution)/shard_map/reshape | solution.py:48
  37.0 3.9 %add_convert_fusion = bf16[2,64,8192]{2,1,0:T(8,128)(2,1)S(1)} fusion(f32[2,64,8192]{2,1,0:T(8,128)} %reshape.33, f32[2,64,8192]{2,1,0:T(8,128)} %concatenate.36), kind=kLoop, calls=%fused_computation.17 | loop fusion | flops 2097152 | bytes 10485760 | tf_op jit(solution)/shard_map/convert_element_type | solution.py:58
  40.9 0.7 fusion.38
  41.5 0.7 fusion.37
  42.2 0.7 fusion.36
  42.9 0.7 fusion.35
  43.5 0.7 fusion.34
  44.2 0.7 fusion.33
  50.8 0.7 fusion.23
  51.5 6.6 %all-to-all-start = ((bf16[16,2,64,512]{3,2,1,0:T(8,128)(2,1)}), bf16[16,2,64,512]{3,2,1,0:T(8,128)(2,1)S(1)}, u32[]{:S(2)}, u32[]{:S(2)}) async-start(bf16[16,2,64,512]{3,2,1,0:T(8,128)(2,1)} %fusion.23), calls=%async_computation | async-start | bytes 4194304 | tf_op jit(solution)/shard_map/all_to_all | solution.py:119
  58.1 19.0 %fusion.14 = (bf16[1024,1024]{1,0:T(8,128)(2,1)}, bf16[1024,1024]{1,0:T(8,128)(2,1)}, bf16[1024,1024]{1,0:T(8,128)(2,1)}) fusion(f32[1024]{0:T(1024)S(1)} %multiply_subtract_fusion), kind=kLoop, calls=%fused_computation.24 | loop fusion | flops 20971520 | bytes 6295552 | tf_op jit(solution)/shard_map/convert.5
  77.2 28.3 %all-to-all-done = bf16[16,2,64,512]{3,2,1,0:T(8,128)(2,1)S(1)} async-done(((bf16[16,2,64,512]{3,2,1,0:T(8,128)(2,1)}), bf16[16,2,64,512]{3,2,1,0:T(8,128)(2,1)S(1)}, u32[]{:S(2)}, u32[]{:S(2)}) %all-to-all-start) | async-done | bytes 2097184 | tf_op jit(solution)/shard_map/all_to_all | solution.py:119
  105.6 10.7 %fusion = f32[2048,512]{0,1:T(8,128)S(1)} fusion(bf16[2048,512]{1,0:T(8,128)(2,1)S(1)} %bitcast.82, bf16[1024,1024]{1,0:T(8,128)(2,1)} %get-tuple-element.11, bf16[1024,1024]{1,0:T(8,128)(2,1)} %get-tuple-element.10, bf16[1024,1024]{1,0:T(8,128)(2,1)} %get-tuple-element.9), kind=kOutput, calls=%fused_computation | convolution fusion | flops 4328521728 | bytes 12582912 | tf_op jit(solution)/shard_map/dot_general | solution.py:79
  116.8 1.5 copy-done
  118.3 3.6 %collective-permute-start = (f32[1024,16]{0,1:T(8,128)S(1)}, f32[1024,16]{0,1:T(8,128)S(1)}, u32[]{:S(2)}, u32[]{:S(2)}) collective-permute-start(f32[1024,16]{0,1:T(8,128)S(1)} %get-tuple-element.7), channel_id=1, source_target_pairs={{0,1},{1,2},{2,3},{3,4},{4,5},{5,6},{6,7},{7,8},{8,9},{9,10},{10,1... | collective-permute-start | bytes 196616 | tf_op jit(solution)/shard_map/ppermute | solution.py:21
  121.9 2.1 %collective-permute-start.1 = (f32[1024,16]{0,1:T(8,128)S(1)}, f32[1024,16]{0,1:T(8,128)S(1)}, u32[]{:S(2)}, u32[]{:S(2)}) collective-permute-start(f32[1024,16]{0,1:T(8,128)S(1)} %get-tuple-element.8), channel_id=1, source_target_pairs={{1,0},{2,1},{3,2},{4,3},{5,4},{6,5},{7,6},{8,7},{9,8},{10,9},{11,1... | collective-permute-start | bytes 196616 | tf_op jit(solution)/shard_map/ppermute | solution.py:23
  124.1 4.2 %collective-permute-done.1 = f32[1024,16]{0,1:T(8,128)S(1)} collective-permute-done((f32[1024,16]{0,1:T(8,128)S(1)}, f32[1024,16]{0,1:T(8,128)S(1)}, u32[]{:S(2)}, u32[]{:S(2)}) %collective-permute-start.1) | collective-permute-done | bytes 65568 | tf_op jit(solution)/shard_map/ppermute | solution.py:23
  128.8 1.2 copy-done.1
  130.0 3.2 %concatenate.38 = f32[1032,544]{0,1:T(8,128)S(1)} concatenate(f32[4,544]{0,1:T(8,128)S(1)} %get-tuple-element.6, f32[1024,544]{0,1:T(8,128)} %copy-done.1, f32[4,544]{0,1:T(8,128)S(1)} %get-tuple-element.5), dimensions={0} | concatenate | bytes 4491264 | tf_op jit(solution)/shard_map/concatenate | solution.py:102
  133.2 2.3 %add_add_fusion = f32[1032,512]{0,1:T(8,128)} fusion(f32[1032,544]{0,1:T(8,128)S(1)} %concatenate.38), kind=kLoop, calls=%fused_computation.57 | loop fusion | flops 2113536 | bytes 12681216 | tf_op jit(solution)/shard_map/add | solution.py:87
  135.5 7.7 %slice_add_fusion = f32[1032,512]{0,1:T(8,128)} fusion(f32[1032,544]{0,1:T(8,128)S(1)} %concatenate.38), kind=kLoop, calls=%fused_computation.25 | loop fusion | flops 16908288 | bytes 71860224 | tf_op jit(solution)/shard_map/add | solution.py:87
  143.2 18.1 %fusion.21 = f32[1024,512]{0,1:T(8,128)S(1)} fusion(f32[1032,512]{0,1:T(8,128)} %add_add_fusion, f32[1032,512]{0,1:T(8,128)} %slice_add_fusion, f32[512]{0:T(512)S(1)} %multiply_subtract_fusion.1, f32[2048,512]{0,1:T(8,128)} %copy-done), kind=kLoop, calls=%fused_computation.61 | loop fusion | flops 8388608 | bytes 31459328 | tf_op jit(solution)/shard_map/div | solution.py:114
  161.3 1.8 %copy.9 = f32[1024,512]{1,0:T(8,128)} copy(f32[1024,512]{0,1:T(8,128)S(1)} %fusion.21) | data formatting | bytes 4194304 | tf_op jit(solution)/shard_map/div | solution.py:114
  (29 shorter events, 8.6 us)
Async XLA Ops:
  51.5 54.0 %all-to-all-start = ((bf16[16,2,64,512]{3,2,1,0:T(8,128)(2,1)}), bf16[16,2,64,512]{3,2,1,0:T(8,128)(2,1)S(1)}, u32[]{:S(2)}, u32[]{:S(2)}) async-start(bf16[16,2,64,512]{3,2,1,0:T(8,128)(2,1)} %fusion.23), calls=%async_computation | async-start | bytes 4194304 | tf_op jit(solution)/shard_map/all_to_all | solution.py:119
  116.3 1.9 %copy-start = (f32[2048,512]{0,1:T(8,128)}, f32[2048,512]{0,1:T(8,128)S(1)}, u32[]{:S(2)}) copy-start(f32[2048,512]{0,1:T(8,128)S(1)} %fusion) | copy-start | bytes 12582916
  118.3 5.8 %collective-permute-start = (f32[1024,16]{0,1:T(8,128)S(1)}, f32[1024,16]{0,1:T(8,128)S(1)}, u32[]{:S(2)}, u32[]{:S(2)}) collective-permute-start(f32[1024,16]{0,1:T(8,128)S(1)} %get-tuple-element.7), channel_id=1, source_target_pairs={{0,1},{1,2},{2,3},{3,4},{4,5},{5,6},{6,7},{7,8},{8,9},{9,10},{10,1... | collective-permute-start | bytes 196616 | tf_op jit(solution)/shard_map/ppermute | solution.py:21
  121.9 6.5 %collective-permute-start.1 = (f32[1024,16]{0,1:T(8,128)S(1)}, f32[1024,16]{0,1:T(8,128)S(1)}, u32[]{:S(2)}, u32[]{:S(2)}) collective-permute-start(f32[1024,16]{0,1:T(8,128)S(1)} %get-tuple-element.8), channel_id=1, source_target_pairs={{1,0},{2,1},{3,2},{4,3},{5,4},{6,5},{7,6},{8,7},{9,8},{10,9},{11,1... | collective-permute-start | bytes 196616 | tf_op jit(solution)/shard_map/ppermute | solution.py:23
  128.6 1.4 copy-start.1
